TPU v7x, 512 devices: a whole 4x8x8 slice. The times are simulated.
512 devices in a mesh: edge: 8 (over x, core), frame: 64 (over y, z).
Axes of the slice: x: 4, y: 8, z: 8, core: 2. Of those that a mesh axis runs over, the one named last changes fastest.
Arguments:
- inv_depth: float32 [2048, 1280], P('frame'), may hold values from 0.3 to 2
- poses: float32 [6, 2048], P(None, 'frame'), may hold values from -1.2 to 1.2
- targets: int32 [2048, 8], P('frame'), may hold values from 0 to 2047, as said below
- degree: int32 [2048], P('frame'), may hold values from 2 to 8, as said below
- flow: bfloat16 [2048, 8, 2, 1280], P('frame', 'edge'), may hold values from -6 to 6
- confidence: bfloat16 [2048, 8, 1280], P('frame', 'edge'), may hold values from 0.099609375 to 1
- damping_index: int32 [1], replicated, may hold values from 4096 to 4159
- panel_index: int32 [1], replicated, may hold values from 0 to 255
Outputs:
- panel: float32 [12288, 48], P(('edge', 'frame'))
- updated_rhs: float32 [12288], P(('edge', 'frame'))
Inputs may be any that keep to these rules, and one draw needn't show every extreme that they name: `targets`: row i names 8 different keyframes, none of them i; every keyframe is named in exactly 8 slots over all rows. Slots 0 to degree - 1 of a keyframe are edges, the others are empty; some keyframe fills all 8.
All inputs are finite; a program needn't handle non-finite values.
Results may differ from a plain program's by a relative error of at most 0.0005.
Values may be sent and summed in bfloat16 or wider, within the bound.
No kernel may reach another device: no remote copies, remote signals or barrier semaphores. Data moves between devices by JAX's collectives and lax.ppermute only.
A program may use at most 64 MiB of HBM per device.

v0:
```python
import jax
import jax.numpy as jnp
from jax import lax
from jax.sharding import PartitionSpec as P

COLS = 80
PANEL_F = 8


PRECISE = lax.Precision.HIGHEST


def pixel_grid(pixels):
    pixel_index = jnp.arange(pixels, dtype=jnp.int32)
    pixel_column = (pixel_index % COLS).astype(jnp.float32)
    pixel_row = (pixel_index // COLS).astype(jnp.float32)
    image_rows = pixels // COLS
    horizontal = (pixel_column - 0.5 * (COLS - 1)) / (0.5 * COLS)
    vertical = (pixel_row - 0.5 * (image_rows - 1)) / (0.5 * COLS)
    return (horizontal, vertical)


def damping_value(damping_index):
    level = (damping_index[0] - 4096).astype(jnp.float32)
    return 0.3 * jnp.exp(0.05 * level)


def edge_terms(motion, inv_depth, flow, confidence, live_mask, horizontal, vertical, factor):
    across = jnp.broadcast_to(horizontal, confidence.shape)
    upward = jnp.broadcast_to(vertical, confidence.shape)
    nothing = jnp.zeros_like(inv_depth)
    horiz_jacobian = jnp.stack(
        [
            -inv_depth,
            nothing,
            across * inv_depth,
            across * upward,
            -(1.0 + across * across),
            upward,
        ],
        axis=2,
    )
    vert_jacobian = jnp.stack(
        [nothing, -inv_depth, upward * inv_depth, 1.0 + upward * upward, -across * upward, -across],
        axis=2,
    )
    horiz_pred = jnp.sum(horiz_jacobian * motion[:, :, :, None], axis=2)
    vert_pred = jnp.sum(vert_jacobian * motion[:, :, :, None], axis=2)
    flow_float = flow.astype(jnp.float32)
    horiz_resid = flow_float[:, :, 0, :] - horiz_pred
    vert_resid = flow_float[:, :, 1, :] - vert_pred
    horiz_slope = motion[:, :, 2:3] * across - motion[:, :, 0:1]
    vert_slope = motion[:, :, 2:3] * upward - motion[:, :, 1:2]
    weight = confidence.astype(jnp.float32) * live_mask[:, :, None] * factor
    hessian = jnp.einsum(
        "fskp,fslp->fskl", horiz_jacobian * weight[:, :, None, :], horiz_jacobian, precision=PRECISE
    )
    hessian = hessian + jnp.einsum(
        "fskp,fslp->fskl", vert_jacobian * weight[:, :, None, :], vert_jacobian, precision=PRECISE
    )
    gradient = jnp.sum(
        (horiz_jacobian * horiz_resid[:, :, None, :] + vert_jacobian * vert_resid[:, :, None, :])
        * weight[:, :, None, :],
        axis=3,
    )
    cross = (
        horiz_jacobian * horiz_slope[:, :, None, :] + vert_jacobian * vert_slope[:, :, None, :]
    ) * weight[:, :, None, :]
    curvature = weight * (horiz_slope * horiz_slope + vert_slope * vert_slope)
    depth_grad = weight * (horiz_slope * horiz_resid + vert_slope * vert_resid)
    return (hessian, gradient, cross, curvature, depth_grad)


def panel_columns(targets, own_frames, panel_first, panel_width):
    components = jnp.arange(6, dtype=jnp.int32)
    places = jnp.arange(panel_width, dtype=jnp.int32)
    target_cols = (targets[:, :, None] - panel_first) * 6 + components
    own_cols = (own_frames[:, None] - panel_first) * 6 + components
    mapping = (target_cols[:, :, :, None] == places).astype(jnp.float32)
    return mapping - (own_cols[:, None, :, None] == places).astype(jnp.float32)


def assemble(row_blocks, reduced_grad, slot_targets, own_frames, total_rows):
    components = jnp.arange(6, dtype=jnp.int32)
    target_rows = (slot_targets[:, :, None] * 6 + components).reshape(-1)
    own_rows = (own_frames[:, None] * 6 + components).reshape(-1)
    panel_width = row_blocks.shape[-1]
    column = jnp.zeros((total_rows, panel_width), jnp.float32)
    column = column.at[target_rows].add(row_blocks.reshape(-1, panel_width))
    column = column.at[own_rows].add(-jnp.sum(row_blocks, axis=1).reshape(-1, panel_width))
    right_side = jnp.zeros((total_rows,), jnp.float32)
    right_side = right_side.at[target_rows].add(reduced_grad.reshape(-1))
    right_side = right_side.at[own_rows].add(-jnp.sum(reduced_grad, axis=1).reshape(-1))
    return (column, right_side)


def finish(corner, corner_rhs, block_rows, block_rhs):
    chol_lower = jnp.linalg.cholesky(corner)
    panel = jax.scipy.linalg.solve_triangular(chol_lower, block_rows.T, lower=True).T
    solved = jax.scipy.linalg.solve_triangular(chol_lower, corner_rhs, lower=True)
    updated = block_rhs - jnp.dot(panel, solved, precision=PRECISE)
    return (panel, updated)


def per_device(inv_depth, poses, targets, degree, flow, confidence, damping_index, panel_index):
    frames_here, pixels = inv_depth.shape
    slots_here = flow.shape[1]
    slot_count = targets.shape[1]
    edge_place = lax.axis_index("edge")
    frame_place = lax.axis_index("frame")
    frame_total = frames_here * lax.axis_size("frame")
    factor = 4.0 / pixels
    damping = damping_value(damping_index)
    horizontal, vertical = pixel_grid(pixels)
    all_poses = lax.all_gather(poses, "frame", axis=1, tiled=True)
    own_frames = frame_place * frames_here + jnp.arange(frames_here, dtype=jnp.int32)
    slot_first = edge_place * slots_here
    slot_ids = slot_first + jnp.arange(slots_here, dtype=jnp.int32)
    local_targets = lax.dynamic_slice_in_dim(targets, slot_first, slots_here, 1)
    live_mask = (slot_ids[None, :] < degree[:, None]).astype(jnp.float32)
    motion = (
        jnp.transpose(jnp.take(all_poses, local_targets, axis=1), (1, 2, 0)) - poses.T[:, None, :]
    )
    hessian, gradient, cross, curvature, depth_grad = edge_terms(
        motion, inv_depth[:, None, :], flow, confidence, live_mask, horizontal, vertical, factor
    )
    curv_total, grad_total = (
        lax.psum(jnp.sum(curvature, axis=1).astype(jnp.bfloat16), "edge").astype(jnp.float32),
        lax.psum(jnp.sum(depth_grad, axis=1).astype(jnp.bfloat16), "edge").astype(jnp.float32),
    )
    damped = (1.0 + damping) * curv_total + 0.05 * damping * factor
    inverse = 1.0 / damped
    weighted = inverse * grad_total
    cross_hat = cross.astype(jnp.bfloat16)
    panel_first = panel_index[0] * PANEL_F
    panel_width = 6 * PANEL_F
    mapping = panel_columns(targets, own_frames, panel_first, panel_width)
    slot_onehot = (slot_ids[:, None] == jnp.arange(slot_count, dtype=jnp.int32)[None, :]).astype(
        jnp.float32
    )
    own_hat = lax.optimization_barrier(cross_hat).astype(jnp.float32)
    scaled = own_hat * inverse[:, None, None, :]
    part_schur = jnp.einsum(
        "fakp,fblp->fakbl",
        scaled,
        lax.all_gather(cross_hat, "edge", axis=1, tiled=True).astype(jnp.float32),
        precision=PRECISE,
    )
    diag_part = jnp.einsum("ab,fakl->fakbl", slot_onehot, hessian, precision=PRECISE)
    reduced_grad = gradient - jnp.einsum("fakp,fp->fak", own_hat, weighted, precision=PRECISE)
    row_blocks = jnp.einsum("fakbl,fblc->fakc", diag_part - part_schur, mapping, precision=PRECISE)
    total_rows = 6 * frame_total
    column, right_side = assemble(row_blocks, reduced_grad, local_targets, own_frames, total_rows)
    rows_here = total_rows // (lax.axis_size("edge") * lax.axis_size("frame"))
    row_first = (edge_place * lax.axis_size("frame") + frame_place) * rows_here
    diag_cols = jnp.arange(panel_width, dtype=jnp.int32)
    column, right_side = lax.psum((column, right_side), ("edge", "frame"))
    column = column.at[panel_first * 6 + diag_cols, diag_cols].add(damping)
    corner = lax.dynamic_slice_in_dim(column, panel_first * 6, panel_width, 0)
    corner_rhs = lax.dynamic_slice_in_dim(right_side, panel_first * 6, panel_width, 0)
    block_rows = lax.dynamic_slice_in_dim(column, row_first, rows_here, 0)
    block_rhs = lax.dynamic_slice_in_dim(right_side, row_first, rows_here, 0)
    return finish(corner, corner_rhs, block_rows, block_rhs)


def solution(mesh):
    placed = (
        P("frame", None),
        P(None, "frame"),
        P("frame", None),
        P("frame"),
        P("frame", "edge", None, None),
        P("frame", "edge", None),
        P(),
        P(),
    )
    return jax.shard_map(
        per_device,
        mesh=mesh,
        in_specs=placed,
        out_specs=(P(("edge", "frame"), None), P(("edge", "frame"))),
        check_vma=False,
    )
```

profile of v0, /device:TPU:1, one launch (start us, length us, event | category | flops | bytes accessed | tf_op | source)
XLA Modules:
  0.0 546.2 jit_solution(17994128414580420234)
XLA Ops:
  7.4 0.7 compare_convert_fusion.1
  8.0 0.7 and_bitcast_fusion
  8.7 0.8 copy.41
  9.6 45.3 %all-gather = f32[64,32,6]{1,2,0:T(8,128)S(1)} all-gather(f32[1,32,6]{1,2,0:T(8,128)S(1)} %copy.42), channel_id=1, replica_groups=mesh['edge'=8,'frame'=64] {'frame'}, dimensions={0}, use_global_device_ids=true | all-gather | bytes 49920 | tf_op jit(solution)/shard_map/all_gather | solution.py:115
  54.9 0.9 copy_convert_fusion
  55.8 0.5 copy.43
  56.3 0.6 gather_fusion
  56.9 0.2 slice_reduce_fusion.1
  57.1 0.7 bitcast_dynamic-update-slice_fusion.3
  57.8 0.7 multiply_bitcast_fusion.1
  58.5 0.2 copy.36
  58.7 0.2 copy.35
  58.9 0.7 broadcast_dynamic-update-slice_fusion.7
  59.6 0.7 bitcast_dynamic-update-slice_fusion.1
  60.3 0.7 bitcast_dynamic-update-slice_fusion
  60.9 0.1 stack.63
  61.1 0.8 broadcast_dynamic-update-slice_fusion.4
  61.9 0.1 broadcast_in_dim.39
  62.0 0.1 stack.56
  62.1 0.1 stack_broadcast_in_dim.8
  62.2 0.1 broadcast.798
  62.3 1.8 stack.57
  64.1 0.7 stack.64
  64.8 0.7 stack.66
  65.6 0.7 stack.65
  66.3 3.3 stack.67
  69.6 0.9 multiply_reduce_fusion.2
  70.5 0.9 fusion.54
  71.7 1.6 multiply_reduce_fusion
  73.3 0.9 copy.44
  74.2 0.5 all-reduce.4.cloned.1.call-start
  76.2 0.1 add.330
  76.4 0.1 add.306
  76.5 0.7 broadcast_dynamic-update-slice_fusion.2
  77.2 0.7 broadcast_dynamic-update-slice_fusion.1
  77.9 0.7 broadcast_dynamic-update-slice_fusion
  78.5 1.6 broadcast_multiply_fusion.1
  80.2 3.1 fusion.5
  83.3 3.0 fusion.28
  86.3 0.3 copy.40
  86.7 0.1 fusion.50
  86.8 62.3 %all-reduce.6.cloned.1.call-done = (bf16[32,1280]{1,0:T(8,128)(2,1)}, bf16[32,1280]{1,0:T(8,128)(2,1)}) async-done(((bf16[32,1280]{1,0:T(8,128)(2,1)}, bf16[32,1280]{1,0:T(8,128)(2,1)}), (bf16[32,1280]{1,0:T(8,128)(2,1)}, bf16[32,1280]{1,0:T(8,128)(2,1)})) %all-reduce.6.cloned.1.call-update) | async-done | bytes 163856 | tf_op jit(solution)/shard_map/psum | solution.py:128
  149.1 1.0 multiply_bitcast_fusion
  150.0 37.3 %all-gather.3.cloned.1.call-done = bf16[32,8,6,1280]{3,0,2,1:T(8,128)(2,1)} async-done(((bf16[32,1,6,1280]{3,0,2,1:T(8,128)(2,1)}), bf16[32,8,6,1280]{3,0,2,1:T(8,128)(2,1)}) %all-gather.3.cloned.1.call-update) | async-done | bytes 3932176 | tf_op jit(solution)/shard_map/all_gather | solution.py:146
  187.4 28.2 %fusion.23 = f32[32,6,8,6]{2,1,3,0:T(8,128)S(1)} fusion(bf16[32,8,6,1280]{3,0,2,1:T(8,128)(2,1)} %all-gather.3.cloned.1.call-done, bf16[32,1,6,1280]{3,2,0,1:T(8,128)(2,1)S(1)} %get-tuple-element.14, f32[32,1280]{1,0:T(8,128)S(1)} %get-tuple-element.27, f32[8]{0:T(128)S(1)} %compare_convert_fusion, f32[32,6,6]{1,2,0:T(8,128)S(1)} %copy.40), kind=kOutput, calls=%fused_computation.25 | convolution fusion | flops 142067712 | bytes 4629024 | tf_op jit(solution)/shard_map/fakp,fblp->fakbl/dot_general | solution.py:143
  215.6 1.4 convolution_bitcast_fusion
  217.0 4.4 scatter_custom_fusion
  221.5 6.9 %scatter_custom_fusion.1 = f32[12288,48]{1,0:T(8,128)} fusion(f32[12288,48]{1,0:T(8,128)} %scatter_custom_fusion, s32[192]{0:T(256)S(1)} %bitcast.166, f32[192,48]{1,0:T(8,128)S(1)} %reshape.1252), kind=kCustom, calls=%fused_computation.72 | custom fusion | flops 18432 | bytes 2457600 | tf_op jit(solution)/shard_map/scatter-add | solution.py:90
  228.4 1.3 fusion.36
  229.8 0.1 reshape.1274
  229.9 1.8 scatter_custom_fusion.3
  231.7 1.9 scatter_fusion.1
  233.7 100.5 %psum.31 = f32[12288]{0:T(1024)S(1)} all-reduce(f32[12288]{0:T(1024)S(1)} %scatter_fusion.1), channel_id=1, replica_groups=mesh['edge'=8,'frame'=64] {'edge','frame'}, use_global_device_ids=true, to_apply=%region_13.14 | all-reduce | flops 12288 | bytes 98304 | tf_op jit(solution)/shard_map/psum | solution.py:157
  334.2 186.9 %all-reduce.4.cloned.1.call-done = f32[12288,48]{1,0:T(8,128)} async-done(((f32[12288,48]{1,0:T(8,128)}), f32[12288,48]{1,0:T(8,128)}) %all-reduce.4.cloned.1.call-update) | async-done | bytes 2359312 | tf_op jit(solution)/shard_map/psum | solution.py:157
  521.1 4.4 copy.47
  525.5 3.1 scatter_fusion
  528.8 0.1 fusion.59
  528.8 4.4 cholesky.16
  533.3 0.6 compare_reduce_fusion
  533.9 0.7 fusion.55
  534.6 3.7 custom-call.10
  538.2 0.3 fusion.57
  538.6 0.2 convolution_bitcast_fusion.2
  538.8 0.7 fusion.33
  (47 shorter events, 1.1 us)
Async XLA Ops:
  7.2 50.0 %copy-start = (f32[32,1280]{1,0:T(8,128)S(1)}, f32[32,1280]{1,0:T(8,128)}, u32[]{:S(2)}) copy-start(f32[32,1280]{1,0:T(8,128)} %param.8) | copy-start | bytes 491524
  7.2 141.9 %all-reduce.6.cloned.1.call-start = ((), (), s32[]{:S(2)}) async-start(), calls=%async_computation.2 | async-start | bytes 327680 | tf_op jit(solution)/shard_map/psum | solution.py:128
  60.9 1.2 copy-start.1
  69.6 0.9 copy-start.2
  71.5 115.9 %all-gather.3.cloned.1.call-start = ((), (), s32[]{:S(2)}) async-start(), calls=%async_computation | async-start | bytes 4423680 | tf_op jit(solution)/shard_map/all_gather | solution.py:146
  73.3 2.7 copy-start.4
  74.2 446.9 %all-reduce.4.cloned.1.call-start = ((), (), s32[]{:S(2)}) async-start(), calls=%async_computation.1 | async-start | bytes 12582912 | tf_op jit(solution)/shard_map/psum | solution.py:157
  538.5 0.9 copy-start.3
Sparse Core Ops, SparseCore 0:
  71.6 77.4 all-reduce.5
  151.2 36.1 all-gather.2
  228.5 292.5 all-reduce.3
where the time goes:
time: 552 us; the launch traced here: 546 us
  waiting for transfers between devices  287 us (52%)
  blocking collectives  146 us (26%)
  other arithmetic  39.4 us (7%)
  matrix products  38.2 us (7%)
  local copies, waits for them, and re-layouts  19.9 us (4%)
  between operations  15.7 us (3%)
    psum x1, waiting for transfers between devices, per_device(): column, right_side = lax.psum((column, right_side), ('edge', 'frame'))  187 us
    psum x1, blocking collectives, per_device(): column, right_side = lax.psum((column, right_side), ('edge', 'frame'))  101 us
    psum x1, waiting for transfers between devices, per_device(): lax.psum(jnp.sum(curvature, axis=1).astype(jnp.bfloat16), 'edge')  62.3 us
    all_gather x1, blocking collectives, per_device(): all_poses = lax.all_gather(poses, 'frame', axis=1, tiled=True)  45.3 us
    all_gather x1, waiting for transfers between devices, per_device(): lax.all_gather(cross_hat, 'edge', axis=1, tiled=True).astype(jnp.float32)  37.3 us
    dot_general x1, matrix products, per_device(): jnp.einsum('fakp,fblp->fakbl', scaled, lax.all_gather(cross_hat, 'edge',...  28.2 us
  transfers between devices with their start and end apart: 3, of which 3 were waited for; matrix products, arithmetic and copies ran while one was open for 4% of the time, Pallas kernels for 0%

commit v1 on v0

v1 whole, which is shorter than its diff:
```python
import numpy as np
import jax
import jax.numpy as jnp
from jax import lax
from jax.experimental import pallas as pl
from jax.experimental.pallas import tpu as pltpu
from jax.sharding import PartitionSpec as P

COLS = 80
PANEL_F = 8
PIXELS = 1280
SLOTS = 8
OWN = 4
FACTOR = 4.0 / PIXELS
PITCH = 42
STEP = 8
INTERPRET = False
F32 = jnp.float32
BF16 = jnp.bfloat16
HIGH = lax.Precision.HIGHEST

VMEM = pl.BlockSpec(memory_space=pltpu.VMEM)
SMEM = pl.BlockSpec(memory_space=pltpu.SMEM)


def basis_rows():
    p = np.arange(PIXELS)
    x = ((p % COLS).astype(np.float32) - np.float32(0.5 * (COLS - 1))) / np.float32(0.5 * COLS)
    rows = PIXELS // COLS
    y = ((p // COLS).astype(np.float32) - np.float32(0.5 * (rows - 1))) / np.float32(0.5 * COLS)
    x = x.astype(np.float64)
    y = y.astype(np.float64)
    r2 = x * x + y * y
    out = np.zeros((16, PIXELS))
    out[:12] = [
        np.ones(PIXELS), x, y, r2, x * y, 1 + x * x, 1 + y * y, y * (1 + r2), x * (1 + r2),
        x * x * y * y + (1 + y * y) ** 2, x * y * (2 + r2), (1 + x * x) ** 2 + x * x * y * y,
    ]
    return out.astype(np.float32)


def moment_map():
    one, x, y, r2, xy, xx1, yy1, yr, xr, h44, h45, h55 = range(12)
    m = np.zeros((128, 128), np.float32)

    def hess(block, row, k, l, sign):
        m[16 * block + row, 6 * k + l] = sign
        m[16 * block + row, 6 * l + k] = sign

    for row, k, l, sign in [(one, 0, 0, 1), (one, 1, 1, 1), (x, 0, 2, -1), (y, 1, 2, -1), (r2, 2, 2, 1)]:
        hess(0, row, k, l, sign)
    for row, k, l, sign in [(xy, 0, 3, -1), (xx1, 0, 4, 1), (y, 0, 5, -1), (yy1, 1, 3, -1), (xy, 1, 4, 1),
                            (x, 1, 5, 1), (yr, 2, 3, 1), (xr, 2, 4, -1)]:
        hess(1, row, k, l, sign)
    for row, k, l, sign in [(h44, 3, 3, 1), (h45, 3, 4, -1), (x, 3, 5, -1), (h55, 4, 4, 1), (y, 4, 5, -1),
                            (r2, 5, 5, 1)]:
        hess(2, row, k, l, sign)
    for block, row, c, sign in [(3, one, 0, -1), (4, one, 1, -1), (3, x, 2, 1), (4, y, 2, 1), (5, xy, 3, 1),
                                (6, yy1, 3, 1), (5, xx1, 4, -1), (6, xy, 4, -1), (5, y, 5, 1), (6, x, 5, -1)]:
        m[16 * block + row, 64 + c] = sign
    return m


def slot_map():
    m = np.zeros((384, 1024), np.float32)
    for k in range(6):
        for l in range(6):
            for b in range(8):
                m[64 * k + 8 * l + b, 128 * b + 6 * k + l] = 1
        m[64 * k + 48, 64 + k] = 1
    return m


def rank_map():
    return np.triu(np.ones((256, 256), np.float32), 1)


def column_map():
    m = np.zeros((3, 128, 384), np.float32)
    for g in range(3):
        for q in range(8):
            for l in range(6):
                for k in range(6):
                    m[g, PITCH * g + 6 * k + l, 48 * k + 6 * q + l] = 1
                m[g, PITCH * g + 37 + l % 3, 288 + 6 * q + l] = 1
    return m


def row_map():
    m = np.zeros((80, 112), np.float32)
    for k in range(6):
        for q in range(8):
            m[6 * q + k, 16 * k + q] = 1
        for r in range(4):
            m[48 + 6 * r + k, 16 * k + 8 + r] = 1
    m[72, 16 * 6 + 12:16 * 6 + 14] = 1
    return m


def lane_codes():
    m = -np.ones((8, 384), np.float32)
    for k in range(7):
        for q in range(8):
            for l in range(6):
                m[0, 48 * k + 6 * q + l] = q
                if k == 6:
                    m[1, 48 * k + 6 * q + l] = l // 3
    return m


def iota(shape, dim, dtype=jnp.int32):
    out = lax.broadcasted_iota(jnp.int32, shape, dim)
    return out if dtype == jnp.int32 else out.astype(dtype)


def thirds(x):
    a = x.astype(BF16)
    r = x - a.astype(F32)
    b = r.astype(BF16)
    return a, b, (r - b.astype(F32)).astype(BF16)


def dot(a, b):
    return lax.dot_general(a, b, (((1,), (0,)), ((), ())), preferred_element_type=F32)


def dot_lanes(a, b, precision=None):
    return lax.dot_general(a, b, (((1,), (1,)), ((), ())), precision=precision, preferred_element_type=F32)


def damping_of(didx_ref):
    level = (didx_ref[0] - 4096).astype(F32)
    return 0.3 * jnp.exp(0.05 * jnp.full((8, 128), level, F32))[0:1, 0:1]


def edge_kernel(ids, pidx, didx, degree, g_ref, d_ref, inv_ref, basis_ref, mmap_ref, smap_ref, rank_ref,
                out_ref, raw_ref, scl_ref, gram_ref, mom_ref, bst_ref):
    e = ids[0]
    f = ids[1]
    pf = pidx[0] * PANEL_F
    pff = pf.astype(F32)
    lane = iota((8, 128), 1)
    sub = iota((8, 128), 0)
    damping = damping_of(didx)

    names = jnp.concatenate([g_ref[pl.ds(0, 64, 4), :], g_ref[pl.ds(1, 64, 4), :]], axis=1)
    frame_row = iota((64, 256), 0)
    here = jnp.sum(jnp.where(frame_row == f, names, 0.0), axis=0, keepdims=True)
    local = names - pff
    earlier = jnp.where(frame_row < f, local, -1.0)
    named = jnp.where(here - pff == iota((8, 256), 0, F32), 1.0, 0.0)
    counts = jnp.concatenate(
        [jnp.sum(jnp.where(earlier == float(q), 1.0, 0.0), axis=0, keepdims=True) for q in range(8)], axis=0)
    rank = dot(named, rank_ref[...]) + jnp.sum(counts, axis=1, keepdims=True)
    slots = jnp.sum(named * (8.0 * iota((8, 256), 0, F32) + rank + 1.0), axis=0, keepdims=True) - 1.0
    row256 = iota((256, 256), 0)
    col256 = iota((256, 256), 1)
    pick = ((row256 & 31) == e * OWN + ((col256 >> 3) & 3)) & ((row256 >> 5) == (col256 >> 5))
    slots = dot(jnp.broadcast_to(slots, (8, 256)), pick.astype(F32))[0:1]
    slots = slots.astype(jnp.int32)
    lane256 = iota((1, 256), 1)
    lane128 = iota((1, 128), 1)
    own_q = f * 32 + e * OWN + (lane128 >> 3) - pf
    own_ok = (lane128 < 32) & (own_q >= 0) & (own_q < 8)

    lane256s = iota((8, 256), 1)
    tcols = [jnp.sum(jnp.where(lane256s == iota((8, 256), 0) * 32 + (e * OWN + i), here, 0.0), axis=1, keepdims=True)
             for i in range(OWN)]
    tcol = jnp.concatenate(tcols, axis=0)
    ocol = (f * 32 + e * OWN + (iota((32, 1), 0) >> 3)).astype(F32)
    both = jnp.concatenate([tcol, ocol], axis=0)
    chunk = jnp.floor(both * (1.0 / 32.0))
    within = both - 32.0 * chunk
    hot = (iota((64, 64), 1, F32) == chunk).astype(F32).astype(BF16)
    poses = jnp.concatenate([g_ref[pl.ds(2, 64, 4), :], g_ref[pl.ds(3, 64, 4), :]], axis=1)
    poses = sum(dot(hot, part) for part in thirds(poses))
    lane64 = iota((64, 256), 1, F32)
    motions = []
    for c in range(6):
        val = jnp.sum(jnp.where(lane64 == 32.0 * c + within, poses, 0.0), axis=1, keepdims=True)
        motions.append(val[0:32] - val[32:64])

    x = basis_ref[1:2, :]
    y = basis_ref[2:3, :]
    xy = basis_ref[4:5, :]
    xx1 = basis_ref[5:6, :]
    yy1 = basis_ref[6:7, :]
    basis = basis_ref[...]
    scl_ref[56:64, :] = jnp.zeros((8, PIXELS), F32)
    mom_ref[...] = jnp.zeros((32, 128), F32)
    for i in range(OWN):
        t1, t2, t3, w1, w2, w3 = [m[8 * i:8 * i + 8] for m in motions]
        d = inv_ref[pl.ds(e * OWN + i, 1), :]
        live = jnp.where(iota((8, 1), 0) < degree[e * OWN + i], 1.0, 0.0)
        weight = d_ref[3 * i + 2] * (live * FACTOR)
        sh = t3 * x - t1
        sv = t3 * y - t2
        rh = d_ref[3 * i] - (d * sh + xy * w1 - xx1 * w2 + y * w3)
        rv = d_ref[3 * i + 1] - (d * sv + yy1 * w1 - xy * w2 - x * w3)
        wsh = weight * sh
        wsv = weight * sv
        curvature = jnp.sum(wsh * sh + wsv * sv, axis=0, keepdims=True)
        slope_grad = jnp.sum(wsh * rh + wsv * rv, axis=0, keepdims=True)
        damped = (1.0 + damping) * curvature + (0.05 * FACTOR) * damping
        inverse = 1.0 / damped
        raw_ref[0:8, :] = -d * wsh
        raw_ref[8:16, :] = -d * wsv
        raw_ref[16:24, :] = d * (x * wsh + y * wsv)
        raw_ref[24:32, :] = xy * wsh + yy1 * wsv
        raw_ref[32:40, :] = -(xx1 * wsh + xy * wsv)
        raw_ref[40:48, :] = y * wsh - x * wsv
        hat = raw_ref[...].astype(BF16)
        scl_ref[0:48, :] = hat.astype(F32) * inverse
        scl_ref[48:56, :] = jnp.broadcast_to(inverse * slope_grad, (8, PIXELS))
        scl = scl_ref[...]
        high = scl.astype(BF16)
        low = (scl - high.astype(F32)).astype(BF16)
        gram = dot_lanes(hat, high) + dot_lanes(hat, low)
        for k in range(6):
            gram_ref[8 * i:8 * i + 8, 64 * k:64 * k + 64] = gram[8 * k:8 * k + 8, :]
        wd = weight * d
        wrh = weight * rh
        wrv = weight * rv
        rows = jnp.concatenate([wd * d, wd, weight, d * wrh, d * wrv, wrh, wrv], axis=0)
        mom = dot_lanes(rows, basis, HIGH)
        for k in range(7):
            mom_ref[8 * i:8 * i + 8, 16 * k:16 * k + 16] = mom[8 * k:8 * k + 8, :]

    hess = sum(dot(part, mmap_ref[...]) for part in thirds(mom_ref[...]))
    gram = sum(dot(part, smap_ref[...]) for part in thirds(gram_ref[...]))
    lane32 = iota((32, 128), 1)
    sub32 = iota((32, 128), 0)
    slot32 = sub32 & 7
    reduced = jnp.where((lane32 >= 64) & (lane32 < 70), hess - gram[:, 0:128], 0.0)
    first = pltpu.roll(reduced, 128 - 27, 1)
    second = pltpu.roll(reduced, 128 - 30, 1)
    ids_block = jnp.where(lane32 == 36, tcol, jnp.where(lane32 == 40, ocol, 0.0))
    own_block = jnp.zeros((32, 128), F32)
    grad_lanes = (lane32 >= 37) & (lane32 < 40)
    for b in range(8):
        block = jnp.where(slot32 == b, hess, 0.0) - gram[:, 128 * b:128 * b + 128]
        block = jnp.where(lane32 < 36, block, 0.0)
        lift = jnp.concatenate(
            [jnp.where(sub == 0, first[8 * i + b:8 * i + b + 1, :], second[8 * i + b:8 * i + b + 1, :])
             for i in range(OWN)], axis=0)
        block = block + jnp.where(grad_lanes & (slot32 < 2), lift, 0.0)
        own_block = own_block - block
        bst_ref[32 * b:32 * b + 32, :] = block + ids_block
    bst_ref[256:288, :] = own_block + ids_block
    bst_ref[288:384, :] = jnp.zeros((96, 128), F32)

    qn = slots >> 3
    jn = slots & 7
    gn = (jn >= 3).astype(jnp.int32) + (jn >= 6).astype(jnp.int32)
    an = lane256 & 7
    row_n = qn * 24 + (jn - 3 * gn) * 8 + an
    row_o = own_q * 24 + 16 + (lane128 & 7)
    stack = bst_ref[...]
    rows192 = iota((192, 384), 0)
    records = jnp.zeros((192, 128), F32)
    for g in range(3):
        naming = jnp.where((slots >= 0) & (gn == g), row_n, -1)
        owning = jnp.where(own_ok, row_o, -1) if g == 2 else jnp.full((1, 128), -1, jnp.int32)
        code = jnp.concatenate([naming, owning], axis=1)
        choose = (rows192 == code).astype(F32).astype(BF16)
        shifted = pltpu.roll(stack, PITCH * g, 1) if g else stack
        for part in thirds(shifted):
            records = records + dot(choose, part)

    lift8 = (lane == sub + 64).astype(F32)
    rg = dot_lanes(lift8, reduced, HIGH)
    frames = iota((32, 2048), 1).astype(F32)
    spread = ((frames == tcol).astype(F32) - (frames == ocol).astype(F32)).astype(BF16)
    rhs = sum(dot(jnp.concatenate([part.astype(F32), jnp.zeros((8, 32), F32)], axis=0).astype(BF16), spread)[0:8]
              for part in thirds(rg))
    for q in range(8):
        out_ref[q, 0:24, :] = records[24 * q:24 * q + 24, :]
        out_ref[q, 24:32, :] = rhs[:, 256 * q:256 * q + 128]
        out_ref[q, 32:40, :] = rhs[:, 256 * q + 128:256 * q + 256]


def edge_stage(ids, pidx, didx, degree, gathered, data, inv_depth):
    consts = (jnp.asarray(basis_rows()), jnp.asarray(moment_map(), BF16), jnp.asarray(slot_map(), BF16),
              jnp.asarray(rank_map()))
    return pl.pallas_call(
        edge_kernel,
        out_shape=on_chip((8, 40, 128)),
        in_specs=[SMEM] * 4 + [VMEM] * 7,
        out_specs=VMEM,
        scratch_shapes=[
            pltpu.VMEM((48, PIXELS), F32), pltpu.VMEM((64, PIXELS), F32), pltpu.VMEM((32, 384), F32),
            pltpu.VMEM((32, 128), F32),
            pltpu.VMEM((384, 128), F32),
        ],
        name="edge_stage",
        interpret=INTERPRET,
    )(ids, pidx, didx, degree, near(gathered), near(data), near(inv_depth), *[near(c) for c in consts])


def on_chip(shape):
    return jax.ShapeDtypeStruct(shape, F32) if INTERPRET else pltpu.VMEM(shape, F32)


def near(x):
    return x if INTERPRET else pltpu.with_memory_space_constraint(x, pltpu.VMEM)


def total(ref):
    out = ref[0]
    for k in range(1, 8):
        out = out + ref[k]
    return out


def sum_edge_kernel(in_ref, out_ref):
    s = total(in_ref)
    for k in range(8):
        out_ref[k, 0:24, :] = s[0:24]
        out_ref[k, 24:32, :] = s[24 + 8 * (k // 4):32 + 8 * (k // 4)]


def sum_y_kernel(in_ref, out_ref):
    s = total(in_ref)
    for k in range(8):
        out_ref[k] = s


def sum_z_kernel(in_ref, out_ref, rhs_ref):
    s = total(in_ref)
    for k in range(8):
        out_ref[k] = s[0:24]
    rhs_ref[...] = s[24:32]


def small_call(kernel, shapes, name, *args):
    return pl.pallas_call(
        kernel,
        out_shape=[on_chip(s) for s in shapes],
        in_specs=[VMEM] * len(args),
        out_specs=[VMEM] * len(shapes),
        name=name,
        interpret=INTERPRET,
    )(*[near(a) for a in args])


def finish_kernel(ids, pidx, didx, r_ref, rb_ref, cmap_ref, rmap_ref, code_ref, panel_ref, upd_ref, cst_ref):
    e = ids[0]
    f = ids[1]
    pf = pidx[0] * PANEL_F
    own0 = (e * 64 + f) * OWN
    damping = damping_of(didx)
    r = r_ref[...].reshape(192, 128)
    rid = iota((128, 1), 0) & 15
    rho = jnp.where(rid < 8, pf + rid, own0 + rid - 8).astype(F32)
    recs = iota((1, 192), 1)
    half = jnp.where((rid - 12) == (recs & 7), 1.0, 0.0)
    mine = jnp.floor((recs.astype(F32) + 0.5) * (1.0 / 24.0)) == (iota((128, 1), 0) >> 4).astype(F32)
    parts = thirds(r)
    c = jnp.zeros((128, 384), F32)
    idrow = iota((16, 128), 0)
    idlane = jnp.where(idrow < 3, PITCH * idrow + 36, PITCH * (idrow - 3) + 40)
    find = ((iota((16, 128), 1) == idlane) & (idrow < 6)).astype(F32).astype(BF16)
    names = sum(dot_lanes(find, part) for part in parts)
    for g in range(3):
        w = jnp.where(names[g:g + 1] == rho, 1.0, 0.0) - jnp.where(names[g + 3:g + 4] == rho, 1.0, 0.0)
        w = jnp.where(mine, jnp.where(rid < 12, w, half), 0.0).astype(BF16)
        picked = sum(dot(w, part) for part in parts)
        c = c + sum(dot(part, cmap_ref[g]) for part in thirds(picked))
    qlane = code_ref[0:1, :]
    alane = code_ref[1:2, :]
    keep = (qlane == (iota((128, 1), 0) >> 4).astype(F32)) & ((alane < 0.0) | (alane == (rid - 12).astype(F32)))
    c = jnp.sum(jnp.where(keep, c, 0.0).reshape(8, 16, 384), axis=0)
    lane16 = iota((16, 128), 1)
    for k in range(7):
        turned = pltpu.roll(c, 384 - 48 * k, 1) if k else c
        cst_ref[16 * k:16 * k + 16, :] = jnp.where(lane16 < 48, turned[:, 0:128], 0.0)
    a = sum(dot(rmap_ref[...], part) for part in thirds(cst_ref[...]))
    row = iota((80, 128), 0)
    lane = iota((80, 128), 1)
    shift = 6 * (own0 - pf) - 48
    diag = ((row < 48) & (lane == row)) | ((row >= 48) & (row < 72) & (lane == row + shift) & (lane < 48))
    a = a + jnp.where(diag, damping, 0.0)
    lane1 = iota((1, 128), 1)
    dvec = jnp.ones((1, 128), F32)
    for start in range(0, 48, STEP):
        cols = [jnp.broadcast_to(a[:, j:j + 1], a.shape) for j in range(start, start + STEP)]
        for m in range(STEP):
            j = start + m
            pivot = cols[m][m:m + 1, :]
            dvec = jnp.where(lane1 == j, pivot, dvec)
            inverse = 1.0 / pivot
            line = jnp.where(lane1 > j, a[m:m + 1, :] * inverse, 0.0)
            for n in range(m + 1, STEP):
                cols[n] = cols[n] - cols[m] * (cols[n][m:m + 1, :] * inverse)
            a = a - cols[m] * line
        a = a[STEP:]
    scale = 1.0 / jnp.sqrt(dvec)
    a = a * scale
    panel = a[0:24]
    panel_ref[...] = panel[:, 0:48]
    z = a[24:25]
    lane24 = iota((24, 128), 1)
    row24 = iota((24, 128), 0)
    r24 = (row24 >= 6).astype(jnp.int32) + (row24 >= 12).astype(jnp.int32) + (row24 >= 18).astype(jnp.int32)
    first = ((f >> 3) & 3) * 32 + (f & 7) * 4
    rb = rb_ref[...]
    rb24 = jnp.concatenate([rb[0:6], rb[0:6], rb[0:6], rb[0:6]], axis=0)
    mixed = jnp.where(lane24 == first + r24, rb24, 0.0) - panel * z
    upd_ref[...] = dot_lanes(jnp.ones((8, 128), F32), mixed, HIGH)[0:1]


def finish_stage(ids, pidx, didx, records, rhs):
    consts = (jnp.asarray(column_map(), BF16), jnp.asarray(row_map(), BF16), jnp.asarray(lane_codes()))
    return pl.pallas_call(
        finish_kernel,
        out_shape=[jax.ShapeDtypeStruct((24, 48), F32), jax.ShapeDtypeStruct((1, 24), F32)],
        in_specs=[SMEM] * 3 + [VMEM] * 5,
        out_specs=[VMEM, VMEM],
        scratch_shapes=[pltpu.VMEM((112, 128), F32)],
        name="finish_stage",
        interpret=INTERPRET,
    )(ids, pidx, didx, near(records), near(rhs), *[near(c) for c in consts])


def graph_kernel(targets_ref, poses_ref, out_ref):
    rows = [targets_ref[k:k + 1, :].astype(F32) for k in range(8)]
    rows += [poses_ref[k:k + 1, :] for k in range(6)] + [jnp.zeros((1, 32), F32)] * 2
    tile = jnp.concatenate([jnp.concatenate(rows[4 * k:4 * k + 4], axis=1) for k in range(4)] * 2, axis=0)
    out_ref[...] = jnp.broadcast_to(tile[None], (32, 8, 128)).reshape(256, 128)


def graph_message(poses, targets):
    return pl.pallas_call(
        graph_kernel,
        out_shape=on_chip((256, 128)),
        in_specs=[VMEM, VMEM],
        out_specs=VMEM,
        name="graph_message",
        interpret=INTERPRET,
    )(targets.T, poses)


def data_message(flow, confidence):
    frames = flow.shape[0]
    both = jnp.concatenate([flow[:, 0], confidence], axis=1)
    return both.reshape(8, frames // 8 * 3, PIXELS)


def data_layout(received):
    return jnp.transpose(received, (1, 0, 2)).astype(F32)


def per_device(inv_depth, poses, targets, degree, flow, confidence, damping_index, panel_index):
    e = lax.axis_index("edge")
    f = lax.axis_index("frame")
    ids = jnp.stack([e, f]).astype(jnp.int32)
    along_y = [[8 * y + z for y in range(8)] for z in range(8)]
    along_z = [[8 * y + z for z in range(8)] for y in range(8)]

    def exchange(x, axis, groups=None):
        return lax.all_to_all(x, axis, 0, 0, axis_index_groups=groups)

    gathered = exchange(graph_message(poses, targets).reshape(64, 4, 128), "frame")
    gathered, raw = lax.optimization_barrier((gathered, data_message(flow, confidence)))
    gathered = gathered.reshape(256, 128)
    data = data_layout(exchange(raw, "edge"))
    part = edge_stage(ids, panel_index, damping_index, degree, gathered, data, inv_depth)
    part = exchange(part, "edge")
    (part,) = small_call(sum_edge_kernel, [(8, 32, 128)], "sum_edge", part)
    part = exchange(part, "frame", along_y)
    (part,) = small_call(sum_y_kernel, [(8, 32, 128)], "sum_y", part)
    part = exchange(part, "frame", along_z)
    records, rhs = small_call(sum_z_kernel, [(8, 24, 128), (8, 128)], "sum_z", part)
    records = exchange(records, "edge")
    panel, updated = finish_stage(ids, panel_index, damping_index, records, rhs)
    return panel, updated.reshape(24)


def solution(mesh):
    placed = (
        P("frame", None),
        P(None, "frame"),
        P("frame", None),
        P("frame"),
        P("frame", "edge", None, None),
        P("frame", "edge", None),
        P(),
        P(),
    )
    return jax.shard_map(
        per_device,
        mesh=mesh,
        in_specs=placed,
        out_specs=(P(("edge", "frame"), None), P(("edge", "frame"))),
        check_vma=False,
    )
```

time: 552 us -> 93.9 us (0.17)
  waiting for transfers between devices: 287 us -> 14.5 us
  blocking collectives: 146 us -> 40.4 us
  other arithmetic: 39.4 us -> 1 us
  matrix products: 38.2 us -> 0 us
  starting transfers between devices: 0.59 us -> 23.7 us
  local copies, waits for them, and re-layouts: 19.9 us -> 1.88 us
  between operations: 15.7 us -> 2.06 us
  Pallas kernels: 0 us -> 9.76 us
    psum x2 -> x0, waiting for transfers between devices: 249 us -> none  [the longest x1 187 us: per_device(): column, right_side = lax.psum((column, right_side), ('edge', 'frame'))]
    psum x1 -> x0, blocking collectives: 101 us -> none  [per_device(): column, right_side = lax.psum((column, right_side), ('edge', 'frame'))]
    all_gather x1 -> x0, blocking collectives: 45.3 us -> none  [per_device(): all_poses = lax.all_gather(poses, 'frame', axis=1, tiled=True)]
    all_to_all x0 -> x4, blocking collectives: none -> 40.4 us  [exchange(): return lax.all_to_all(x, axis, 0, 0, axis_index_groups=groups)]
    dot_general x6 -> x0, matrix products: 37.7 us -> none  [the longest x1 28.2 us: per_device(): jnp.einsum('fakp,fblp->fakbl', scaled, lax.all_gather(cross_hat, 'edge',...]
    all_gather x1 -> x0, waiting for transfers between devices: 37.3 us -> none  [per_device(): lax.all_gather(cross_hat, 'edge', axis=1, tiled=True).astype(jnp.float32)]
    all_to_all x0 -> x2, starting transfers between devices: none -> 23.7 us  [exchange(): return lax.all_to_all(x, axis, 0, 0, axis_index_groups=groups)]
    scatter-add x5 -> x0, other arithmetic: 18.2 us -> none  [the longest x1 6.9 us: assemble(): column.at[own_rows]]
  transfers between devices with their start and end apart: 3 -> 2, of which waited for: 3 -> 2; matrix products, arithmetic and copies ran while one was open for 4% -> 2% of each run, Pallas kernels for 0% -> 0%
where the time goes in v1:
time: 93.9 us; the launch traced here: 93.3 us
  blocking collectives  40.4 us (43%)
  starting transfers between devices  23.7 us (25%)
  waiting for transfers between devices  14.5 us (15%)
  Pallas kernels  9.76 us (10%)
  between operations  2.06 us (2%)
  local copies, waits for them, and re-layouts  1.88 us (2%)
  other arithmetic  1 us (1%)
    all_to_all x4, blocking collectives, exchange(): return lax.all_to_all(x, axis, 0, 0, axis_index_groups=groups)  40.4 us
    all_to_all x2, starting transfers between devices, exchange(): return lax.all_to_all(x, axis, 0, 0, axis_index_groups=groups)  23.7 us
    all_to_all x2, waiting for transfers between devices, exchange(): return lax.all_to_all(x, axis, 0, 0, axis_index_groups=groups)  14.5 us
    pallas_call x1, Pallas kernels, edge_stage(): pl.pallas_call(edge_kernel, out_shape=on_chip((8, 40, 128)), in_specs=[SM...  4.38 us
    pallas_call x1, Pallas kernels, finish_stage(): pl.pallas_call(finish_kernel, out_shape=[jax.ShapeDtypeStruct((24, 48), F...  3.89 us
  transfers between devices with their start and end apart: 2, of which 2 were waited for; matrix products, arithmetic and copies ran while one was open for 2% of the time, Pallas kernels for 0%

profile of v1, /device:TPU:1, one launch (start us, length us, event | category | flops | bytes accessed | tf_op | source)
XLA Modules:
  0.0 93.3 jit_solution(8868803072759809552)
XLA Ops:
  0.6 1.4 %graph_message.1 = f32[256,128]{1,0:T(8,128)} custom-call(s32[8,32]{1,0:T(8,128)} %bitcast.11, f32[6,32]{1,0:T(8,128)} %poses_ref.1), custom_call_target="tpu_custom_call" | custom-call | tf_op jit(solution)/shard_map/graph_message/pallas_call | solution.py:433
  2.1 0.0 copy-start.9
  2.1 17.3 %all-to-all-start = ((f32[64,4,128]{2,1,0:T(4,128)}), f32[64,4,128]{2,1,0:T(4,128)S(1)}, u32[]{:S(2)}, u32[]{:S(2)}) async-start(f32[64,4,128]{2,1,0:T(4,128)} %bitcast.3), calls=%async_computation | async-start | bytes 262144 | tf_op jit(solution)/shard_map/all_to_all | solution.py:461
  19.3 0.0 copy-done.9
  19.3 0.0 copy-start.8
  19.4 0.1 copy.20
  19.5 0.8 copy-done.8
  20.3 0.3 pad_maximum_fusion
  20.6 0.9 reshape.17
  21.5 0.0 copy-start
  21.5 9.3 %all-to-all-done = f32[64,4,128]{2,1,0:T(4,128)S(1)} async-done(((f32[64,4,128]{2,1,0:T(4,128)}), f32[64,4,128]{2,1,0:T(4,128)S(1)}, u32[]{:S(2)}, u32[]{:S(2)}) %all-to-all-start) | async-done | bytes 131104 | tf_op jit(solution)/shard_map/all_to_all | solution.py:461
  30.8 6.5 %all-to-all-start.1 = ((bf16[8,12,1280]{2,1,0:T(8,128)(2,1)}), bf16[8,12,1280]{2,1,0:T(8,128)(2,1)S(1)}, u32[]{:S(2)}, u32[]{:S(2)}) async-start(bf16[8,12,1280]{2,1,0:T(8,128)(2,1)} %reshape.17), calls=%async_computation.1 | async-start | bytes 655360 | tf_op jit(solution)/shard_map/all_to_all | solution.py:461
  38.6 0.6 pad_add_fusion.ids
  39.2 0.0 copy-start.2
  39.2 0.0 copy-start.3
  39.2 0.0 copy-start.4
  39.2 0.0 copy-start.5
  39.2 5.2 %all-to-all-done.1 = bf16[8,12,1280]{2,1,0:T(8,128)(2,1)S(1)} async-done(((bf16[8,12,1280]{2,1,0:T(8,128)(2,1)}), bf16[8,12,1280]{2,1,0:T(8,128)(2,1)S(1)}, u32[]{:S(2)}, u32[]{:S(2)}) %all-to-all-start.1) | async-done | bytes 245792 | tf_op jit(solution)/shard_map/all_to_all | solution.py:461
  44.4 0.1 convert_bitcast_fusion.d_ref
  44.5 0.0 copy-done
  44.5 0.0 copy-done.2
  44.5 0.0 copy-done.3
  44.5 0.0 copy-done.4
  44.5 0.0 copy-done.5
  44.5 4.4 %edge_stage.1 = f32[8,40,128]{2,1,0:T(8,128)S(1)} custom-call(s32[2]{0:T(128)} %pad_add_fusion.ids, s32[1]{0:T(128)S(6)} %copy.24.pidx, s32[1]{0:T(128)S(6)} %copy.23.didx, s32[32]{0:T(128)} %degree.1, f32[256,128]{1,0:T(8,128)S(1)} %bitcast.9, f32[12,8,1280]{2,1,0:T(8,128)S(1)} %convert_bitcast_fusion.d_ref, f32[32,1280]{1,0:T(8,128)S(1)} %copy-done.3, ...), custom_call_target="tpu_custom_call" | custom-call | tf_op jit(solution)/shard_map/edge_stage/pallas_call | solution.py:285
  48.9 9.1 %all_to_all.30.in_ref = f32[8,40,128]{2,1,0:T(8,128)S(1)} all-to-all(f32[8,40,128]{2,1,0:T(8,128)S(1)} %edge_stage.1), channel_id=1, replica_groups=mesh['edge'=8,'frame'=64] {'edge'}, dimensions={0} | all-to-all | bytes 327680 | tf_op jit(solution)/shard_map/all_to_all | solution.py:461
  58.0 10.1 %all_to_all.31.in_ref = f32[8,32,128]{2,1,0:T(8,128)S(1)} all-to-all(f32[8,32,128]{2,1,0:T(8,128)S(1)} %sum_edge.1), channel_id=1, replica_groups={{0,8,16,24,32,40,48,56},{1,9,17,25,33,41,49,57},{2,10,18,26,34,42,50,58..., dimensions={0} | all-to-all | bytes 262144 | tf_op jit(solution)/shard_map/all_to_all | solution.py:461
  68.1 0.0 copy-start.1
  68.2 10.5 %all_to_all.32.in_ref = f32[8,32,128]{2,1,0:T(8,128)S(1)} all-to-all(f32[8,32,128]{2,1,0:T(8,128)S(1)} %sum_y.1), channel_id=1, replica_groups={{0,1,2,3,4,5,6,7},{8,9,10,11,12,13,14,15},{16,17,18,19,20,21,22,23},{24..., dimensions={0} | all-to-all | bytes 262144 | tf_op jit(solution)/shard_map/all_to_all | solution.py:461
  78.7 0.0 copy-start.6
  78.7 0.0 copy-start.7
  78.7 10.7 %all_to_all.33.r_ref = f32[8,24,128]{2,1,0:T(8,128)S(1)} all-to-all(f32[8,24,128]{2,1,0:T(8,128)S(1)} %get-tuple-element.10), channel_id=1, replica_groups=mesh['edge'=8,'frame'=64] {'edge'}, dimensions={0} | all-to-all | bytes 196608 | tf_op jit(solution)/shard_map/all_to_all | solution.py:461
  89.4 0.0 copy-done.1
  89.4 0.0 copy-done.6
  89.4 0.0 copy-done.7
  89.4 3.9 %finish_stage.1 = (f32[24,48]{1,0:T(8,128)}, f32[1,24]{1,0:T(1,128)}) custom-call(s32[2]{0:T(128)} %pad_add_fusion.ids, s32[1]{0:T(128)S(6)} %copy.24.pidx, s32[1]{0:T(128)S(6)} %copy.23.didx, f32[8,24,128]{2,1,0:T(8,128)S(1)} %all_to_all.33.r_ref, f32[8,128]{1,0:T(8,128)S(1)} %get-tuple-element.11.rb_ref, bf16[3,128,384]{2,1,0:T(8,128)(2,1)S(1)} %copy-done.1, ...), custom_call_target="tpu_custom_call" | custom-call | tf_op jit(solution)/shard_map/finish_stage/pallas_call | solution.py:414
  (3 shorter events, 0.0 us)
Async XLA Ops:
  2.1 17.3 %copy-start.9 = (bf16[32,1,1280]{2,0,1:T(8,128)(2,1)S(1)}, bf16[32,1,1280]{2,0,1:T(8,128)(2,1)}, u32[]{:S(2)}) copy-start(bf16[32,1,1280]{2,0,1:T(8,128)(2,1)} %param.20) | copy-start | bytes 245764
  2.1 28.8 %all-to-all-start = ((f32[64,4,128]{2,1,0:T(4,128)}), f32[64,4,128]{2,1,0:T(4,128)S(1)}, u32[]{:S(2)}, u32[]{:S(2)}) async-start(f32[64,4,128]{2,1,0:T(4,128)} %bitcast.3), calls=%async_computation | async-start | bytes 262144 | tf_op jit(solution)/shard_map/all_to_all | solution.py:461
  19.3 0.9 copy-start.8
  21.5 22.9 %copy-start = (bf16[384,1024]{1,0:T(8,128)(2,1)S(1)}, bf16[384,1024]{1,0:T(8,128)(2,1)}, u32[]{:S(2)}) copy-start(bf16[384,1024]{1,0:T(8,128)(2,1)} %constant.25.clone.smap_ref) | copy-start | bytes 2359300
  30.8 13.5 %all-to-all-start.1 = ((bf16[8,12,1280]{2,1,0:T(8,128)(2,1)}), bf16[8,12,1280]{2,1,0:T(8,128)(2,1)S(1)}, u32[]{:S(2)}, u32[]{:S(2)}) async-start(bf16[8,12,1280]{2,1,0:T(8,128)(2,1)} %reshape.17), calls=%async_computation.1 | async-start | bytes 655360 | tf_op jit(solution)/shard_map/all_to_all | solution.py:461
  39.2 5.3 %copy-start.2 = (f32[256,256]{1,0:T(8,128)S(1)}, f32[256,256]{1,0:T(8,128)}, u32[]{:S(2)}) copy-start(f32[256,256]{1,0:T(8,128)} %constant.26.clone.rank_ref) | copy-start | bytes 786436
  39.2 5.3 %copy-start.3 = (f32[32,1280]{1,0:T(8,128)S(1)}, f32[32,1280]{1,0:T(8,128)}, u32[]{:S(2)}) copy-start(f32[32,1280]{1,0:T(8,128)} %inv_ref.1) | copy-start | bytes 491524
  39.2 5.3 %copy-start.4 = (f32[16,1280]{1,0:T(8,128)S(1)}, f32[16,1280]{1,0:T(8,128)}, u32[]{:S(2)}) copy-start(f32[16,1280]{1,0:T(8,128)} %constant.23.clone.basis_ref) | copy-start | bytes 245764
  39.2 5.3 %copy-start.5 = (bf16[128,128]{1,0:T(8,128)(2,1)S(1)}, bf16[128,128]{1,0:T(8,128)(2,1)}, u32[]{:S(2)}) copy-start(bf16[128,128]{1,0:T(8,128)(2,1)} %constant.24.clone.mmap_ref) | copy-start | bytes 98308
  68.1 21.3 %copy-start.1 = (bf16[3,128,384]{2,1,0:T(8,128)(2,1)S(1)}, bf16[3,128,384]{2,1,0:T(8,128)(2,1)}, u32[]{:S(2)}) copy-start(bf16[3,128,384]{2,1,0:T(8,128)(2,1)} %constant.27.clone.cmap_ref) | copy-start | bytes 884740
  78.7 10.7 %copy-start.6 = (bf16[80,112]{1,0:T(8,128)(2,1)S(1)}, bf16[80,112]{1,0:T(8,128)(2,1)}, u32[]{:S(2)}) copy-start(bf16[80,112]{1,0:T(8,128)(2,1)} %constant.28.clone.rmap_ref) | copy-start | bytes 53764
  78.7 10.7 %copy-start.7 = (f32[8,384]{1,0:T(8,128)S(1)}, f32[8,384]{1,0:T(8,128)}, u32[]{:S(2)}) copy-start(f32[8,384]{1,0:T(8,128)} %constant.29.clone.code_ref) | copy-start | bytes 36868
